TPU v7x, 128 devices: a whole 4x4x4 slice. The times are simulated.
128 devices in a mesh: packs: 8 (over x, core), seq: 16 (over y, z).
Axes of the slice: x: 4, y: 4, z: 4, core: 2. Of those that a mesh axis runs over, the one named last changes fastest.
Arguments:
- queries: bfloat16 [16384, 8192], P(('packs', 'seq')), parts along dimension 0, may hold values from -12 to 12
- keys: bfloat16 [16384, 1024], P(('packs', 'seq')), parts along dimension 0, may hold values from -6 to 6
- values: bfloat16 [16384, 1024], P(('packs', 'seq')), parts along dimension 0, may hold values from -6 to 6
- outputs: bfloat16 [16384, 8192], P(('packs', 'seq')), parts along dimension 0, may hold values from -6 to 6
- grad_out: bfloat16 [16384, 8192], P(('packs', 'seq')), parts along dimension 0, may hold values from -4 to 4
- lse_saved: float32 [16384, 64], P(('packs', 'seq')), parts along dimension 0, may hold values from -40 to 40
- doc_lengths: int32 [64], P('packs'), parts along dimension 0, may hold values from 1 to 1024, as said below
Outputs:
- grad_queries: bfloat16 [16384, 8192], P(('packs', 'seq')), parts along dimension 0
- grad_keys: bfloat16 [16384, 1024], P(('packs', 'seq')), parts along dimension 0
- grad_values: bfloat16 [16384, 1024], P(('packs', 'seq')), parts along dimension 0
There are 8 independent parts, one for each index of `packs`. A program takes and returns all parts, laid end to end along the dimension named above; each array names one. Nothing has to cross between parts.
Inputs may be any that keep to these rules, and one draw needn't show every extreme that they name: `doc_lengths`: positive lengths summing to 2048; one document has exactly 1024 tokens.
All inputs are finite; a program needn't handle non-finite values.
Results may differ from a plain program's by a relative error of at most 0.0049.
Values may be sent and summed in bfloat16 or wider, within the bound.
A program may use at most 64 MiB of HBM per device.

v0:
```python
import jax
import jax.numpy as jnp
from jax import lax
from jax.sharding import PartitionSpec as P

HEADS = 64
KVH = 8
HDIM = 128


def segment_ids(doc_lengths, total):
    boundary = jnp.cumsum(doc_lengths)
    position = jnp.arange(total, dtype=jnp.int32)
    return jnp.sum((position[:, None] >= boundary[None, :]).astype(jnp.int32), axis=1)


def left_dot(first, second):
    return lax.dot_general(
        first, second, (((0,), (0,)), ((), ())), preferred_element_type=jnp.float32
    )


def right_dot(first, second):
    return lax.dot_general(
        first, second, (((1,), (1,)), ((), ())), preferred_element_type=jnp.float32
    )


def block_terms(
    query_blk,
    gout_blk,
    lse_blk,
    delta_blk,
    query_seg,
    query_pos,
    key_blk,
    value_blk,
    key_seg,
    key_pos,
    scale,
):
    scores = right_dot(query_blk, key_blk) * scale
    visible = (key_pos[None, :] <= query_pos[:, None]) & (key_seg[None, :] == query_seg[:, None])
    attn_prob = jnp.where(visible, jnp.exp(scores - lse_blk[:, None]), 0.0)
    grad_prob = right_dot(gout_blk, value_blk)
    grad_score = (attn_prob * (grad_prob - delta_blk[:, None])).astype(jnp.bfloat16)
    prob_half = attn_prob.astype(jnp.bfloat16)
    grad_query = jnp.dot(grad_score, key_blk, preferred_element_type=jnp.float32) * scale
    grad_key = left_dot(grad_score, query_blk) * scale
    grad_value = left_dot(prob_half, gout_blk)
    return (grad_query, grad_key, grad_value)


def shards(queries, keys, values, outputs, grad_out, lse_saved, doc_lengths):
    seq_size = lax.axis_size("seq")
    local_rows = queries.shape[0]
    total = local_rows * seq_size
    head_dim = HDIM
    heads_here = HEADS // seq_size
    share_count = seq_size // KVH
    scale = 1.0 / head_dim**0.5

    def to_slots(array):
        return array.reshape(local_rows, seq_size, heads_here * head_dim)

    query_heads, out_heads, gout_heads = (
        lax.all_to_all(to_slots(queries), "seq", split_axis=1, concat_axis=0, tiled=True),
        lax.all_to_all(to_slots(outputs), "seq", split_axis=1, concat_axis=0, tiled=True),
        lax.all_to_all(to_slots(grad_out), "seq", split_axis=1, concat_axis=0, tiled=True),
    )
    lse_heads = lax.all_to_all(
        lse_saved.reshape(local_rows, seq_size, heads_here),
        "seq",
        split_axis=1,
        concat_axis=0,
        tiled=True,
    )
    out_heads = out_heads.reshape(total, heads_here, head_dim)
    gout_heads = gout_heads.reshape(total, heads_here, head_dim)
    delta_heads = jnp.einsum(
        "thd,thd->th", out_heads, gout_heads, preferred_element_type=jnp.float32
    )
    query_heads = query_heads.reshape(total, heads_here, head_dim)
    lse_heads = lse_heads.reshape(total, heads_here)
    key_slots = jnp.repeat(keys.reshape(local_rows, KVH, head_dim), share_count, axis=1)
    value_slots = jnp.repeat(values.reshape(local_rows, KVH, head_dim), share_count, axis=1)
    key_heads, value_heads = (
        lax.all_to_all(key_slots, "seq", split_axis=1, concat_axis=0, tiled=True),
        lax.all_to_all(value_slots, "seq", split_axis=1, concat_axis=0, tiled=True),
    )
    key_heads = key_heads.reshape(total, head_dim)
    value_heads = value_heads.reshape(total, head_dim)
    segment = segment_ids(doc_lengths, total)
    position = jnp.arange(total, dtype=jnp.int32)
    block = min(512, total)
    num_blocks = total // block

    def step(carry, index):
        grad_q_all, grad_k_acc, grad_v_acc = carry
        head = index // num_blocks
        start = index % num_blocks * block
        query_blk = lax.dynamic_slice(query_heads, (start, head, 0), (block, 1, head_dim)).reshape(
            block, head_dim
        )
        gout_blk = lax.dynamic_slice(gout_heads, (start, head, 0), (block, 1, head_dim)).reshape(
            block, head_dim
        )
        lse_blk = lax.dynamic_slice(lse_heads, (start, head), (block, 1)).reshape(block)
        delta_blk = lax.dynamic_slice(delta_heads, (start, head), (block, 1)).reshape(block)
        query_seg = lax.dynamic_slice_in_dim(segment, start, block)
        query_pos = lax.dynamic_slice_in_dim(position, start, block)
        grad_query, grad_key, grad_value = block_terms(
            query_blk,
            gout_blk,
            lse_blk,
            delta_blk,
            query_seg,
            query_pos,
            key_heads,
            value_heads,
            segment,
            position,
            scale,
        )
        grad_k_acc = grad_k_acc + grad_key
        grad_v_acc = grad_v_acc + grad_value
        grad_q_all = lax.dynamic_update_slice(
            grad_q_all,
            grad_query.astype(jnp.bfloat16).reshape(block, 1, head_dim),
            (start, head, 0),
        )
        return ((grad_q_all, grad_k_acc, grad_v_acc), None)

    start_carry = (
        jnp.zeros((total, heads_here, head_dim), jnp.bfloat16),
        jnp.zeros((total, head_dim), jnp.float32),
        jnp.zeros((total, head_dim), jnp.float32),
    )
    final_carry, unused = lax.scan(
        step, start_carry, jnp.arange(heads_here * num_blocks, dtype=jnp.int32)
    )
    grad_q_all, grad_k_acc, grad_v_acc = final_carry
    grad_queries = lax.all_to_all(
        grad_q_all.reshape(total, 1, heads_here * head_dim),
        "seq",
        split_axis=0,
        concat_axis=1,
        tiled=True,
    )
    grad_queries = grad_queries.reshape(local_rows, HEADS * head_dim)
    key_back, value_back = (
        lax.all_to_all(
            grad_k_acc.reshape(total, 1, head_dim), "seq", split_axis=0, concat_axis=1, tiled=True
        ),
        lax.all_to_all(
            grad_v_acc.reshape(total, 1, head_dim), "seq", split_axis=0, concat_axis=1, tiled=True
        ),
    )
    grad_keys = (
        jnp.sum(key_back.reshape(local_rows, KVH, share_count, head_dim), axis=2)
        .reshape(local_rows, KVH * head_dim)
        .astype(jnp.bfloat16)
    )
    grad_values = (
        jnp.sum(value_back.reshape(local_rows, KVH, share_count, head_dim), axis=2)
        .reshape(local_rows, KVH * head_dim)
        .astype(jnp.bfloat16)
    )
    return (grad_queries, grad_keys, grad_values)


def solution(mesh):
    placed = (
        P(("packs", "seq"), None),
        P(("packs", "seq"), None),
        P(("packs", "seq"), None),
        P(("packs", "seq"), None),
        P(("packs", "seq"), None),
        P(("packs", "seq"), None),
        P("packs"),
    )
    return jax.shard_map(
        shards,
        mesh=mesh,
        in_specs=placed,
        out_specs=(P(("packs", "seq"), None), P(("packs", "seq"), None), P(("packs", "seq"), None)),
        check_vma=False,
    )
```

profile of v0, /device:TPU:0, one launch (start us, length us, event | category | flops | bytes accessed | tf_op | source)
XLA Modules:
  0.0 481.4 jit_solution(6178511105931249375)
XLA Ops:
  0.7 8.3 %all-to-all-start.2 = ((f32[128,16,4]{0,2,1:T(4,128)}), f32[128,16,4]{0,2,1:T(4,128)S(1)}, u32[]{:S(2)}, u32[]{:S(2)}) async-start(f32[128,16,4]{0,2,1:T(4,128)} %bitcast.141), calls=%async_computation.2 | async-start | bytes 65536 | tf_op jit(solution)/shard_map/all_to_all | solution.py:71
  9.0 7.6 %all-to-all-done.2 = f32[128,16,4]{0,2,1:T(4,128)S(1)} async-done(((f32[128,16,4]{0,2,1:T(4,128)}), f32[128,16,4]{0,2,1:T(4,128)S(1)}, u32[]{:S(2)}, u32[]{:S(2)}) %all-to-all-start.2) | async-done | bytes 32800 | tf_op jit(solution)/shard_map/all_to_all | solution.py:71
  17.5 3.6 all-to-all-start.1
  23.5 7.9 %all-to-all-done.1 = bf16[128,16,128]{2,0,1:T(8,128)(2,1)S(1)} async-done(((bf16[128,16,128]{2,0,1:T(8,128)(2,1)}), bf16[128,16,128]{2,0,1:T(8,128)(2,1)S(1)}, u32[]{:S(2)}, u32[]{:S(2)}) %all-to-all-start.1) | async-done | bytes 524320 | tf_op jit(solution)/shard_map/all_to_all | solution.py:88
  31.4 3.7 all-to-all-start
  35.1 4.1 copy.71
  39.2 23.6 %all-to-all-done = bf16[128,16,512]{0,2,1:T(8,128)(2,1)S(1)} async-done(((bf16[128,16,512]{0,2,1:T(8,128)(2,1)}), bf16[128,16,512]{0,2,1:T(8,128)(2,1)S(1)}, u32[]{:S(2)}, u32[]{:S(2)}) %all-to-all-start) | async-done | bytes 2097184 | tf_op jit(solution)/shard_map/all_to_all | solution.py:67
  64.1 4.4 all-to-all-start.5
  68.6 4.1 copy.68
  72.6 23.6 %all-to-all-done.5 = bf16[128,16,512]{0,2,1:T(8,128)(2,1)} async-done(((bf16[128,16,512]{0,2,1:T(8,128)(2,1)}), bf16[128,16,512]{0,2,1:T(8,128)(2,1)}, u32[]{:S(2)}, u32[]{:S(2)}) %all-to-all-start.5) | async-done | bytes 2097184 | tf_op jit(solution)/shard_map/all_to_all | solution.py:68
  96.3 4.3 all-to-all-start.3
  100.7 27.7 %all-to-all-done.3 = bf16[128,16,512]{0,2,1:T(8,128)(2,1)S(1)} async-done(((bf16[128,16,512]{0,2,1:T(8,128)(2,1)}), bf16[128,16,512]{0,2,1:T(8,128)(2,1)S(1)}, u32[]{:S(2)}, u32[]{:S(2)}) %all-to-all-start.3) | async-done | bytes 2097184 | tf_op jit(solution)/shard_map/all_to_all | solution.py:69
  129.9 4.2 all-to-all-start.4
  134.4 4.3 copy.66
  138.7 4.2 reshape.128
  142.9 4.3 copy.72
  147.2 4.2 reshape.140
  151.4 4.3 copy.69
  155.6 4.1 reshape.135
  159.8 2.9 fusion.16
  164.3 235.0 %while.18 = (s32[]{:T(128)}, bf16[2048,4,128]{0,2,1:T(8,128)(2,1)}, f32[2048,128]{1,0:T(8,128)}, f32[2048,128]{1,0:T(8,128)S(1)}, s32[2048]{0:T(1024)S(1)}, /*in...) while((s32[]{:T(128)}, bf16[2048,4,128]{0,2,1:T(8,128)(2,1)}, ...), condition=%wide.region_3.4_spmd.clone.clone, body=%wide.region_2.3_spmd.clone.clone.sunk | while | flops 1354104832 | bytes 25862684 | solution.py:139
  167.8 2.6 exponential_select_fusion.2
  175.1 2.7 fusion.47
  182.1 2.5 exponential_select_fusion.2
  189.4 3.1 fusion.47
  196.9 2.6 exponential_select_fusion.2
  204.1 3.1 fusion.47
  211.6 2.6 exponential_select_fusion.2
  218.8 3.1 fusion.47
  226.3 2.6 exponential_select_fusion.2
  233.6 3.1 fusion.47
  241.0 2.6 exponential_select_fusion.2
  248.3 3.1 fusion.47
  255.7 2.6 exponential_select_fusion.2
  263.0 3.1 fusion.47
  270.4 2.6 exponential_select_fusion.2
  277.7 3.1 fusion.47
  285.1 2.6 exponential_select_fusion.2
  292.4 3.1 fusion.47
  299.8 2.6 exponential_select_fusion.2
  307.1 3.1 fusion.47
  314.5 2.6 exponential_select_fusion.2
  321.8 3.1 fusion.47
  329.2 2.6 exponential_select_fusion.2
  336.5 3.1 fusion.47
  344.0 2.6 exponential_select_fusion.2
  351.3 3.1 fusion.47
  358.7 2.6 exponential_select_fusion.2
  366.0 3.1 fusion.47
  373.4 2.6 exponential_select_fusion.2
  380.7 3.1 fusion.47
  388.1 2.6 exponential_select_fusion.2
  395.4 3.1 fusion.47
  399.3 21.5 %all_to_all.135 = f32[2048,1,128]{2,1,0:T(1,128)} all-to-all(f32[2048,1,128]{2,1,0:T(1,128)S(1)} %bitcast.123), channel_id=1, replica_groups=mesh['packs'=8,'seq'=16] {'seq'}, dimensions={0} | all-to-all | bytes 2097152 | tf_op jit(solution)/shard_map/all_to_all | solution.py:155
  420.8 4.0 all-to-all-start.7
  425.3 2.9 reduce.2
  428.3 2.9 copy.97
  431.1 2.8 reshape.156
  433.9 4.1 all-to-all-done.7
  438.0 3.7 all-to-all-start.6
  446.8 18.6 %all-to-all-done.6 = bf16[16,2,32768]{2,1,0:T(2,128)(2,1)S(1)} async-done(((bf16[16,2,32768]{2,1,0:T(2,128)(2,1)}), bf16[16,2,32768]{2,1,0:T(2,128)(2,1)S(1)}, u32[]{:S(2)}, u32[]{:S(2)}) %all-to-all-start.6) | async-done | bytes 2097184 | tf_op jit(solution)/shard_map/all_to_all | solution.py:143
  465.5 6.7 %reshape.157 = bf16[2048,1,512]{2,1,0:T(2,128)(2,1)} reshape(bf16[16,2,32768]{2,1,0:T(2,128)(2,1)S(1)} %all-to-all-done.6) | data formatting | bytes 4194304
  472.1 2.8 copy.92
  477.3 4.1 copy.80
  (197 shorter events, 118.1 us)
Async XLA Ops:
  0.6 8.3 %copy-start = (bf16[128,1024]{1,0:T(8,128)(2,1)S(1)}, bf16[128,1024]{1,0:T(8,128)(2,1)}, u32[]{:S(2)}) copy-start(bf16[128,1024]{1,0:T(8,128)(2,1)} %param.10) | copy-start | bytes 786436
  0.6 20.4 %copy-start.5 = (bf16[128,8192]{1,0:T(8,128)(2,1)S(1)}, bf16[128,8192]{1,0:T(8,128)(2,1)}, u32[]{:S(2)}) copy-start(bf16[128,8192]{1,0:T(8,128)(2,1)} %param.9) | copy-start | bytes 6291460
  0.7 15.9 %all-to-all-start.2 = ((f32[128,16,4]{0,2,1:T(4,128)}), f32[128,16,4]{0,2,1:T(4,128)S(1)}, u32[]{:S(2)}, u32[]{:S(2)}) async-start(f32[128,16,4]{0,2,1:T(4,128)} %bitcast.141), calls=%async_computation.2 | async-start | bytes 65536 | tf_op jit(solution)/shard_map/all_to_all | solution.py:71
  17.5 13.9 %all-to-all-start.1 = ((bf16[128,16,128]{2,0,1:T(8,128)(2,1)}), bf16[128,16,128]{2,0,1:T(8,128)(2,1)S(1)}, u32[]{:S(2)}, u32[]{:S(2)}) async-start(bf16[128,16,128]{2,0,1:T(8,128)(2,1)} %bitcast.5), calls=%async_computation.1 | async-start | bytes 1048576 | tf_op jit(solution)/shard_map/all_to_all | solution.py:88
  31.4 31.4 %all-to-all-start = ((bf16[128,16,512]{0,2,1:T(8,128)(2,1)}), bf16[128,16,512]{0,2,1:T(8,128)(2,1)S(1)}, u32[]{:S(2)}, u32[]{:S(2)}) async-start(bf16[128,16,512]{0,2,1:T(8,128)(2,1)} %bitcast.129), calls=%async_computation | async-start | bytes 4194304 | tf_op jit(solution)/shard_map/all_to_all | solution.py:67
  62.8 1.3 copy-start.2
  64.1 32.2 %all-to-all-start.5 = ((bf16[128,16,512]{0,2,1:T(8,128)(2,1)}), bf16[128,16,512]{0,2,1:T(8,128)(2,1)}, u32[]{:S(2)}, u32[]{:S(2)}) async-start(bf16[128,16,512]{0,2,1:T(8,128)(2,1)} %bitcast.130), calls=%async_computation.5 | async-start | bytes 4194304 | tf_op jit(solution)/shard_map/all_to_all | solution.py:68
  96.3 4.4 copy-start.6
  96.3 32.2 %all-to-all-start.3 = ((bf16[128,16,512]{0,2,1:T(8,128)(2,1)}), bf16[128,16,512]{0,2,1:T(8,128)(2,1)S(1)}, u32[]{:S(2)}, u32[]{:S(2)}) async-start(bf16[128,16,512]{0,2,1:T(8,128)(2,1)} %bitcast.131), calls=%async_computation.3 | async-start | bytes 4194304 | tf_op jit(solution)/shard_map/all_to_all | solution.py:69
  100.6 33.5 %copy-start.7 = (s32[8]{0:T(128)S(1)}, s32[8]{0:T(128)}, u32[]{:S(2)}) copy-start(s32[8]{0:T(128)} %param.15) | copy-start | bytes 100
  128.5 1.5 copy-start.3
  129.9 32.8 %all-to-all-start.4 = ((bf16[128,16,128]{2,0,1:T(8,128)(2,1)}), bf16[128,16,128]{2,0,1:T(8,128)(2,1)S(1)}, u32[]{:S(2)}, u32[]{:S(2)}) async-start(bf16[128,16,128]{2,0,1:T(8,128)(2,1)} %bitcast.16), calls=%async_computation.4 | async-start | bytes 1048576 | tf_op jit(solution)/shard_map/all_to_all | solution.py:89
  420.8 4.5 copy-start.4
  420.8 17.2 %all-to-all-start.7 = ((f32[2048,1,128]{2,1,0:T(1,128)}), f32[2048,1,128]{2,1,0:T(1,128)S(1)}, u32[]{:S(2)}, u32[]{:S(2)}) async-start(f32[2048,1,128]{2,1,0:T(1,128)} %bitcast.26), calls=%async_computation.7 | async-start | bytes 2097152 | tf_op jit(solution)/shard_map/all_to_all | solution.py:152
  438.0 27.4 %all-to-all-start.6 = ((bf16[16,2,32768]{2,1,0:T(2,128)(2,1)}), bf16[16,2,32768]{2,1,0:T(2,128)(2,1)S(1)}, u32[]{:S(2)}, u32[]{:S(2)}) async-start(bf16[16,2,32768]{2,1,0:T(2,128)(2,1)} %reshape.156), calls=%async_computation.6 | async-start | bytes 4194304 | tf_op jit(solution)/shard_map/all_to_all | solution.py:143
  477.3 4.1 copy-start.1
where the time goes:
time: 485 us; the launch traced here: 481 us
  matrix products  166 us (34%)
  waiting for transfers between devices  113 us (23%)
  local copies, waits for them, and re-layouts  93.8 us (19%)
  loops' own time  42.5 us (9%)
  starting transfers between devices  36.3 us (7%)
  blocking collectives  21.5 us (4%)
  other arithmetic  7.52 us (2%)
    dot_general x32, matrix products, left_dot(): lax.dot_general(first, second, (((0,), (0,)), ((), ())), preferred_elemen...  83.9 us
    dot_general x32, matrix products, right_dot(): lax.dot_general(first, second, (((1,), (1,)), ((), ())), preferred_elemen...  70.4 us
    another operation x1, loops' own time, shards(): lax.scan(step, start_carry, jnp.arange(heads_here * num_blocks, dtype=jnp...  42.5 us
    unnamed x26, local copies, waits for them, and re-layouts  34.3 us
    all_to_all x1, waiting for transfers between devices, shards(): lax.all_to_all(to_slots(grad_out), 'seq', split_axis=1, concat_axis=0, ti...  27.7 us
    all_to_all x1, waiting for transfers between devices, shards(): lax.all_to_all(to_slots(outputs), 'seq', split_axis=1, concat_axis=0, til...  23.6 us
    all_to_all x1, waiting for transfers between devices, shards(): lax.all_to_all(to_slots(queries), 'seq', split_axis=1, concat_axis=0, til...  23.6 us
    all_to_all x1, blocking collectives, shards(): lax.all_to_all(grad_v_acc.reshape(total, 1, head_dim), 'seq', split_axis=...  21.5 us
  transfers between devices with their start and end apart: 8, of which 7 were waited for; matrix products, arithmetic and copies ran while one was open for 11% of the time, Pallas kernels for 0%

commit v1 on v0

--- a/solution.py
+++ b/solution.py
@@ -64,7 +64,12 @@
         return array.reshape(local_rows, seq_size, heads_here * head_dim)
 
     query_heads, out_heads, gout_heads = (
-        lax.all_to_all(to_slots(queries), "seq", split_axis=1, concat_axis=0, tiled=True),
+        jnp.concatenate(
+            lax.all_to_all(
+                jnp.stack(jnp.split(to_slots(queries), lax.axis_size("seq"), axis=1)), "seq", 0, 0
+            ),
+            axis=0,
+        ),
         lax.all_to_all(to_slots(outputs), "seq", split_axis=1, concat_axis=0, tiled=True),
         lax.all_to_all(to_slots(grad_out), "seq", split_axis=1, concat_axis=0, tiled=True),
     )

time: 485 us -> 494 us (1.019)
  local copies, waits for them, and re-layouts: 93.8 us -> 105 us
  waiting for transfers between devices: 113 us -> 107 us
    unnamed x26 -> x39, local copies, waits for them, and re-layouts: 34.3 us -> 45.1 us
    all_to_all x1, waiting for transfers between devices: 7.56 us -> 0.01 us  [shards(): lax.all_to_all(lse_saved.reshape(local_rows, seq_size, heads_here), 'seq'...]
  transfers between devices with their start and end apart: 8 -> 8, of which waited for: 7 -> 6; matrix products, arithmetic and copies ran while one was open for 11% -> 13% of each run, Pallas kernels for 0% -> 0%
where the time goes in v1:
time: 494 us; the launch traced here: 490 us
  matrix products  166 us (34%)
  waiting for transfers between devices  107 us (22%)
  local copies, waits for them, and re-layouts  105 us (21%)
  loops' own time  42.5 us (9%)
  starting transfers between devices  39.9 us (8%)
  blocking collectives  21.5 us (4%)
  other arithmetic  7.52 us (2%)
    dot_general x32, matrix products, left_dot(): lax.dot_general(first, second, (((0,), (0,)), ((), ())), preferred_elemen...  84 us
    dot_general x32, matrix products, right_dot(): lax.dot_general(first, second, (((1,), (1,)), ((), ())), preferred_elemen...  70.2 us
    unnamed x39, local copies, waits for them, and re-layouts  45.1 us
    another operation x1, loops' own time, shards(): lax.scan(step, start_carry, jnp.arange(heads_here * num_blocks, dtype=jnp...  42.5 us
    all_to_all x1, waiting for transfers between devices, shards(): lax.all_to_all(to_slots(grad_out), 'seq', split_axis=1, concat_axis=0, ti...  27.8 us
    all_to_all x1, waiting for transfers between devices, shards(): lax.all_to_all(jnp.stack(jnp.split(to_slots(queries), lax.axis_size('seq'...  23.7 us
    all_to_all x1, waiting for transfers between devices, shards(): lax.all_to_all(to_slots(outputs), 'seq', split_axis=1, concat_axis=0, til...  23.6 us
    all_to_all x1, blocking collectives, shards(): lax.all_to_all(grad_v_acc.reshape(total, 1, head_dim), 'seq', split_axis=...  21.5 us
  transfers between devices with their start and end apart: 8, of which 6 were waited for; matrix products, arithmetic and copies ran while one was open for 13% of the time, Pallas kernels for 0%

profile of v1, /device:TPU:0, one launch (start us, length us, event | category | flops | bytes accessed | tf_op | source)
XLA Modules:
  0.0 490.2 jit_solution(12479600725891654303)
XLA Ops:
  0.6 8.3 %all-to-all-start.2 = ((f32[128,16,4]{0,2,1:T(4,128)}), f32[128,16,4]{0,2,1:T(4,128)S(1)}, u32[]{:S(2)}, u32[]{:S(2)}) async-start(f32[128,16,4]{0,2,1:T(4,128)} %bitcast.216), calls=%async_computation.2 | async-start | bytes 65536 | tf_op jit(solution)/shard_map/all_to_all | solution.py:76
  9.0 3.2 copy.114
  21.8 7.2 %all-to-all-start.1 = ((bf16[128,16,128]{2,0,1:T(8,128)(2,1)}), bf16[128,16,128]{2,0,1:T(8,128)(2,1)S(1)}, u32[]{:S(2)}, u32[]{:S(2)}) async-start(bf16[128,16,128]{2,0,1:T(8,128)(2,1)} %bitcast.19), calls=%async_computation.1 | async-start | bytes 1048576 | tf_op jit(solution)/shard_map/all_to_all | solution.py:93
  31.0 8.9 %all-to-all-done.1 = bf16[128,16,128]{2,0,1:T(8,128)(2,1)S(1)} async-done(((bf16[128,16,128]{2,0,1:T(8,128)(2,1)}), bf16[128,16,128]{2,0,1:T(8,128)(2,1)S(1)}, u32[]{:S(2)}, u32[]{:S(2)}) %all-to-all-start.1) | async-done | bytes 524320 | tf_op jit(solution)/shard_map/all_to_all | solution.py:93
  39.9 3.7 all-to-all-start
  43.7 4.1 copy.122
  47.8 23.7 %all-to-all-done = bf16[16,128,1,512]{1,3,2,0:T(8,128)(2,1)S(1)} async-done(((bf16[16,128,1,512]{1,3,2,0:T(8,128)(2,1)}), bf16[16,128,1,512]{1,3,2,0:T(8,128)(2,1)S(1)}, u32[]{:S(2)}, u32[]{:S(2)}) %all-to-all-start) | async-done | bytes 2097184 | tf_op jit(solution)/shard_map/all_to_all | solution.py:68
  72.8 4.4 all-to-all-start.5
  77.3 4.1 copy.119
  81.3 23.6 %all-to-all-done.5 = bf16[128,16,512]{0,2,1:T(8,128)(2,1)} async-done(((bf16[128,16,512]{0,2,1:T(8,128)(2,1)}), bf16[128,16,512]{0,2,1:T(8,128)(2,1)}, u32[]{:S(2)}, u32[]{:S(2)}) %all-to-all-start.5) | async-done | bytes 2097184 | tf_op jit(solution)/shard_map/all_to_all | solution.py:73
  105.0 4.3 all-to-all-start.3
  109.4 27.8 %all-to-all-done.3 = bf16[128,16,512]{0,2,1:T(8,128)(2,1)S(1)} async-done(((bf16[128,16,512]{0,2,1:T(8,128)(2,1)}), bf16[128,16,512]{0,2,1:T(8,128)(2,1)S(1)}, u32[]{:S(2)}, u32[]{:S(2)}) %all-to-all-start.3) | async-done | bytes 2097184 | tf_op jit(solution)/shard_map/all_to_all | solution.py:74
  138.6 4.2 all-to-all-start.4
  143.1 4.3 copy.117
  147.4 4.2 reshape_reshape.3
  151.5 4.3 copy.123
  155.8 4.2 reshape.135
  160.0 4.3 copy.120
  164.3 4.2 reshape.130
  168.5 2.9 fusion.16
  173.0 235.0 %while.18 = (s32[]{:T(128)}, bf16[2048,4,128]{0,2,1:T(8,128)(2,1)}, f32[2048,128]{1,0:T(8,128)}, f32[2048,128]{1,0:T(8,128)S(1)}, s32[2048]{0:T(1024)S(1)}, /*in...) while((s32[]{:T(128)}, bf16[2048,4,128]{0,2,1:T(8,128)(2,1)}, ...), condition=%wide.region_3.4_spmd.clone.clone, body=%wide.region_2.3_spmd.clone.clone.sunk | while | flops 1354104832 | bytes 25862684 | solution.py:144
  176.5 2.6 exponential_select_fusion.2
  183.8 2.7 fusion.63
  190.8 2.6 exponential_select_fusion.2
  198.1 3.1 fusion.63
  205.5 2.5 exponential_select_fusion.2
  212.8 3.1 fusion.63
  220.2 2.5 exponential_select_fusion.2
  227.5 3.1 fusion.63
  235.0 2.5 exponential_select_fusion.2
  242.2 3.1 fusion.63
  249.7 2.5 exponential_select_fusion.2
  257.0 3.1 fusion.63
  264.4 2.5 exponential_select_fusion.2
  271.7 3.1 fusion.63
  279.1 2.5 exponential_select_fusion.2
  286.4 3.1 fusion.63
  293.8 2.5 exponential_select_fusion.2
  301.1 3.1 fusion.63
  308.5 2.5 exponential_select_fusion.2
  315.8 3.1 fusion.63
  323.2 2.5 exponential_select_fusion.2
  330.5 3.1 fusion.63
  337.9 2.5 exponential_select_fusion.2
  345.2 3.1 fusion.63
  352.6 2.5 exponential_select_fusion.2
  359.9 3.1 fusion.63
  367.4 2.5 exponential_select_fusion.2
  374.6 3.1 fusion.63
  382.1 2.5 exponential_select_fusion.2
  389.4 3.1 fusion.63
  396.8 2.5 exponential_select_fusion.2
  404.1 3.1 fusion.63
  408.0 21.5 %all_to_all.125 = f32[2048,1,128]{2,1,0:T(1,128)} all-to-all(f32[2048,1,128]{2,1,0:T(1,128)S(1)} %bitcast.184), channel_id=1, replica_groups=mesh['packs'=8,'seq'=16] {'seq'}, dimensions={0} | all-to-all | bytes 2097152 | tf_op jit(solution)/shard_map/all_to_all | solution.py:160
  429.5 4.0 all-to-all-start.7
  434.1 2.9 reduce.2
  437.0 2.9 copy.149
  439.9 2.8 reshape.151
  442.6 4.1 all-to-all-done.7
  446.8 3.7 all-to-all-start.6
  455.6 18.6 %all-to-all-done.6 = bf16[16,2,32768]{2,1,0:T(2,128)(2,1)S(1)} async-done(((bf16[16,2,32768]{2,1,0:T(2,128)(2,1)}), bf16[16,2,32768]{2,1,0:T(2,128)(2,1)S(1)}, u32[]{:S(2)}, u32[]{:S(2)}) %all-to-all-start.6) | async-done | bytes 2097184 | tf_op jit(solution)/shard_map/all_to_all | solution.py:148
  474.2 6.7 %reshape.152 = bf16[2048,1,512]{2,1,0:T(2,128)(2,1)} reshape(bf16[16,2,32768]{2,1,0:T(2,128)(2,1)S(1)} %all-to-all-done.6) | data formatting | bytes 4194304
  480.9 2.8 copy.144
  486.1 4.1 copy.131
  (211 shorter events, 126.4 us)
Async XLA Ops:
  0.6 8.3 %copy-start = (bf16[128,1024]{1,0:T(8,128)(2,1)S(1)}, bf16[128,1024]{1,0:T(8,128)(2,1)}, u32[]{:S(2)}) copy-start(bf16[128,1024]{1,0:T(8,128)(2,1)} %param.10) | copy-start | bytes 786436
  0.6 20.2 %all-to-all-start.2 = ((f32[128,16,4]{0,2,1:T(4,128)}), f32[128,16,4]{0,2,1:T(4,128)S(1)}, u32[]{:S(2)}, u32[]{:S(2)}) async-start(f32[128,16,4]{0,2,1:T(4,128)} %bitcast.216), calls=%async_computation.2 | async-start | bytes 65536 | tf_op jit(solution)/shard_map/all_to_all | solution.py:76
  21.8 18.2 %all-to-all-start.1 = ((bf16[128,16,128]{2,0,1:T(8,128)(2,1)}), bf16[128,16,128]{2,0,1:T(8,128)(2,1)S(1)}, u32[]{:S(2)}, u32[]{:S(2)}) async-start(bf16[128,16,128]{2,0,1:T(8,128)(2,1)} %bitcast.19), calls=%async_computation.1 | async-start | bytes 1048576 | tf_op jit(solution)/shard_map/all_to_all | solution.py:93
  39.9 31.6 %all-to-all-start = ((bf16[16,128,1,512]{1,3,2,0:T(8,128)(2,1)}), bf16[16,128,1,512]{1,3,2,0:T(8,128)(2,1)S(1)}, u32[]{:S(2)}, u32[]{:S(2)}) async-start(bf16[16,128,1,512]{1,3,2,0:T(8,128)(2,1)} %fusion.17), calls=%async_computation | async-start | bytes 4194304 | tf_op jit(solution)/shard_map/all_to_all | solution.py:68
  71.5 1.3 copy-start.2
  72.8 32.1 %all-to-all-start.5 = ((bf16[128,16,512]{0,2,1:T(8,128)(2,1)}), bf16[128,16,512]{0,2,1:T(8,128)(2,1)}, u32[]{:S(2)}, u32[]{:S(2)}) async-start(bf16[128,16,512]{0,2,1:T(8,128)(2,1)} %bitcast.205), calls=%async_computation.5 | async-start | bytes 4194304 | tf_op jit(solution)/shard_map/all_to_all | solution.py:73
  105.0 4.3 copy-start.5
  105.0 32.2 %all-to-all-start.3 = ((bf16[128,16,512]{0,2,1:T(8,128)(2,1)}), bf16[128,16,512]{0,2,1:T(8,128)(2,1)S(1)}, u32[]{:S(2)}, u32[]{:S(2)}) async-start(bf16[128,16,512]{0,2,1:T(8,128)(2,1)} %bitcast.206), calls=%async_computation.3 | async-start | bytes 4194304 | tf_op jit(solution)/shard_map/all_to_all | solution.py:74
  109.3 33.5 %copy-start.6 = (s32[8]{0:T(128)S(1)}, s32[8]{0:T(128)}, u32[]{:S(2)}) copy-start(s32[8]{0:T(128)} %param.15) | copy-start | bytes 100
  137.1 1.5 copy-start.3
  138.6 32.8 %all-to-all-start.4 = ((bf16[128,16,128]{2,0,1:T(8,128)(2,1)}), bf16[128,16,128]{2,0,1:T(8,128)(2,1)S(1)}, u32[]{:S(2)}, u32[]{:S(2)}) async-start(bf16[128,16,128]{2,0,1:T(8,128)(2,1)} %bitcast.30), calls=%async_computation.4 | async-start | bytes 1048576 | tf_op jit(solution)/shard_map/all_to_all | solution.py:94
  429.5 4.5 copy-start.4
  429.5 17.2 %all-to-all-start.7 = ((f32[2048,1,128]{2,1,0:T(1,128)}), f32[2048,1,128]{2,1,0:T(1,128)S(1)}, u32[]{:S(2)}, u32[]{:S(2)}) async-start(f32[2048,1,128]{2,1,0:T(1,128)} %bitcast.40), calls=%async_computation.7 | async-start | bytes 2097152 | tf_op jit(solution)/shard_map/all_to_all | solution.py:157
  446.8 27.4 %all-to-all-start.6 = ((bf16[16,2,32768]{2,1,0:T(2,128)(2,1)}), bf16[16,2,32768]{2,1,0:T(2,128)(2,1)S(1)}, u32[]{:S(2)}, u32[]{:S(2)}) async-start(bf16[16,2,32768]{2,1,0:T(2,128)(2,1)} %reshape.151), calls=%async_computation.6 | async-start | bytes 4194304 | tf_op jit(solution)/shard_map/all_to_all | solution.py:148
  486.1 4.1 copy-start.1
